TPU v7x, 128 devices: a whole 4x4x4 slice. The times are simulated.
128 devices in a mesh: tm: 32 (over x, y, z_hi), tensor: 4 (over z_lo, core).
Axes of the slice: x: 4, y: 4, z: 4 (z_hi: 2, z_lo: 2; z = z_hi * 2 + z_lo), core: 2. Of those that a mesh axis runs over, the one named last changes fastest.
Arguments:
- frames: bfloat16 [16384, 1408], P('tm'), may hold values from -6 to 6
- gain_attn: float32 [1408], replicated, may hold values from 0.25 to 1.75
- w_qkv: bfloat16 [1408, 3, 1408], P('tm', None, 'tensor')
- w_out: bfloat16 [1408, 1408], P('tensor', 'tm'), may hold values from -0.625 to 0.625
- gain_mlp: float32 [1408], replicated, may hold values from 0.25 to 1.75
- w_up: bfloat16 [1408, 6144], P('tm', 'tensor'), may hold values from -0.15625 to 0.15625
- w_down: bfloat16 [6144, 1408], P('tensor', 'tm'), may hold values from -0.078125 to 0.078125
- w_proj: bfloat16 [1408, 4096], P('tm', 'tensor'), may hold values from -0.15625 to 0.15625
- windows: int32 [256, 8], P('tm'), may hold values from 0 to 255, as said below
- pool_map: int32 [16384], P('tm'), may hold values from 0 to 15, as said below
- owners: int32 [4096, 1], P('tm'), may hold values from 0 to 31; in each aligned block of 128 rows (0 to 127, 128 to 255, ...) at most 8 rows name the same one
Outputs:
- received: bfloat16 [32, 256, 4096], P('tm', None, 'tensor')
Inputs may be any that keep to these rules, and one draw needn't show every extreme that they name: `windows`: row b lists 8 different blocks, each in the frame of block b or in the frame just before or just after it; frame f holds blocks 256 / 64 f onward. `pool_map`: in each aligned block of 64 patches every slot value is named by exactly 4 patches. `owners`: among the 128 rows of one index of tm no owner is named more than 8 times.
All inputs are finite; a program needn't handle non-finite values.
Results may differ from a plain program's by a relative error of at most 0.014.
The roundings to bfloat16 on the way count: a program that leaves them out, or rounds other values in their place, can miss the bound.
Values may be sent and summed in bfloat16 or wider, within the bound.
A program may use at most 64 MiB of HBM per device.

v0:
```python
import math
import jax
import jax.numpy as jnp
from jax import lax
from jax.sharding import PartitionSpec as P

D = 1408
HEADS = 16
PATCHES = 256
BLK = 64
WIN = 8
POOL = 4
eps = 1e-06


def with_halo(block, sides, width):
    for axis, dim in sides:
        count = lax.axis_size(axis)
        forward = [(i, i + 1) for i in range(count - 1)]
        backward = [(target, source) for source, target in forward]
        low = lax.ppermute(
            lax.slice_in_dim(block, block.shape[dim] - width, None, axis=dim), axis, forward
        )
        high = lax.ppermute(lax.slice_in_dim(block, 0, width, axis=dim), axis, backward)
        block = jnp.concatenate([low, block, high], axis=dim)
    return block


def layer_norm(values, scales):
    average = jnp.mean(values, axis=-1, keepdims=True)
    centred = values - average
    spread = jnp.mean(centred * centred, axis=-1, keepdims=True)
    return (centred * lax.rsqrt(spread + eps) * scales).astype(jnp.bfloat16)


def pool_rows(values, slot_map):
    block_count = values.shape[0] // BLK
    slot_ids = jnp.arange(BLK // POOL, dtype=jnp.int32)
    chooser = (slot_map.reshape(block_count, 1, BLK) == slot_ids[None, :, None]).astype(jnp.float32)
    summed = jnp.einsum(
        "bsp,bpd->bsd",
        chooser,
        values.reshape(block_count, BLK, values.shape[1]),
        precision=lax.Precision.HIGHEST,
    )
    return (
        (summed * (1.0 / POOL))
        .reshape(block_count * (BLK // POOL), values.shape[1])
        .astype(jnp.bfloat16)
    )


def tensor_total(term):
    return lax.psum(term.astype(jnp.bfloat16), "tensor").astype(jnp.float32)


def body(
    frames, gain_attn, w_qkv, w_out, gain_mlp, w_up, w_down, w_proj, windows, pool_map, owners
):
    row_count = frames.shape[0]
    query_blocks = row_count // BLK
    head_dim = D // HEADS
    full_qkv, full_out, full_up, full_down, full_proj = (
        lax.all_gather(w_qkv, "tm", axis=0, tiled=True),
        lax.all_gather(w_out, "tm", axis=1, tiled=True),
        lax.all_gather(w_up, "tm", axis=0, tiled=True),
        lax.all_gather(w_down, "tm", axis=1, tiled=True),
        lax.all_gather(w_proj, "tm", axis=0, tiled=True),
    )
    local_width = full_qkv.shape[2]
    heads_here = local_width // head_dim
    normed = layer_norm(frames.astype(jnp.float32), gain_attn)
    projected_qkv = jnp.dot(
        normed, full_qkv.reshape(D, 3 * local_width), preferred_element_type=jnp.float32
    ).astype(jnp.bfloat16)
    projected_qkv = projected_qkv.reshape(row_count, 3, local_width)
    keyvals = with_halo(projected_qkv[:, 1:, :], (("tm", 0),), PATCHES)
    per_frame = PATCHES // BLK
    kv_blocks = keyvals.reshape(query_blocks + 2 * per_frame, BLK, 2, heads_here, head_dim)
    local_ids = windows - (lax.axis_index("tm") * query_blocks - per_frame)
    group_size = math.gcd(query_blocks, 8)
    queries = projected_qkv[:, 0, :].reshape(
        query_blocks // group_size, group_size, BLK, heads_here, head_dim
    )
    score_scale = head_dim ** (-0.5)

    def attend_group(packed):
        query_group, id_group = packed
        picked = kv_blocks[id_group].reshape(group_size, WIN * BLK, 2, heads_here, head_dim)
        scores = (
            jnp.einsum(
                "gqhd,gkhd->ghqk", query_group, picked[:, :, 0], preferred_element_type=jnp.float32
            )
            * score_scale
        )
        row_top = jnp.max(scores, axis=-1, keepdims=True)
        expw = jnp.exp(scores - row_top)
        attn_probs = (expw / jnp.sum(expw, axis=-1, keepdims=True)).astype(jnp.bfloat16)
        return jnp.einsum(
            "ghqk,gkhd->gqhd", attn_probs, picked[:, :, 1], preferred_element_type=jnp.float32
        ).astype(jnp.bfloat16)

    attended = lax.map(
        attend_group, (queries, local_ids.reshape(query_blocks // group_size, group_size, WIN))
    ).reshape(row_count, local_width)
    mixed_term = jnp.dot(attended, full_out, preferred_element_type=jnp.float32)
    stream = frames.astype(jnp.float32) + tensor_total(mixed_term)
    hidden = layer_norm(stream, gain_mlp)
    activation = jax.nn.gelu(
        jnp.dot(hidden, full_up, preferred_element_type=jnp.float32), approximate=False
    ).astype(jnp.bfloat16)
    stream = stream + tensor_total(
        jnp.dot(activation, full_down, preferred_element_type=jnp.float32)
    )
    pooled = pool_rows(stream, pool_map)
    proj_rows = jnp.dot(pooled, full_proj, preferred_element_type=jnp.float32).astype(jnp.bfloat16)
    pooled_count = proj_rows.shape[0]
    owner_count = lax.axis_size("tm")
    capacity = 2 * pooled_count // owner_count
    owner_ids = owners[:, 0]
    owner_hits = (owner_ids[:, None] == jnp.arange(owner_count, dtype=jnp.int32)[None, :]).astype(
        jnp.int32
    )
    slot_rank = jnp.sum((jnp.cumsum(owner_hits, axis=0) - 1) * owner_hits, axis=1)
    slot_dest = owner_ids * capacity + slot_rank
    placement = (
        jnp.arange(owner_count * capacity, dtype=jnp.int32)[:, None] == slot_dest[None, :]
    ).astype(jnp.bfloat16)
    outbox = jnp.dot(placement, proj_rows, preferred_element_type=jnp.float32).astype(jnp.bfloat16)
    outbox = outbox.reshape(owner_count, capacity, proj_rows.shape[1])
    received = lax.all_to_all(outbox, "tm", split_axis=0, concat_axis=0, tiled=True)
    return received.reshape(1, owner_count * capacity, proj_rows.shape[1])


def solution(mesh):
    placed = (
        P("tm", None),
        P(),
        P("tm", None, "tensor"),
        P("tensor", "tm"),
        P(),
        P("tm", "tensor"),
        P("tensor", "tm"),
        P("tm", "tensor"),
        P("tm", None),
        P("tm"),
        P("tm", None),
    )
    return jax.shard_map(
        body, mesh=mesh, in_specs=placed, out_specs=P("tm", None, "tensor"), check_vma=False
    )
```

profile of v0, /device:TPU:0, one launch (start us, length us, event | category | flops | bytes accessed | tf_op | source)
XLA Modules:
  0.0 647.8 jit_solution(6431842312539559043)
XLA Ops:
  6.5 1.6 copy.23
  8.1 0.0 all-gather.9.cloned.1.call-update
  8.2 0.0 all-reduce.3.cloned.1.call-start
  8.2 0.7 compare_select_fusion
  8.9 0.1 reshape.80
  9.0 1.6 convert_reduce_fusion
  10.6 1.9 fusion.16
  12.5 83.1 %all-gather.9.cloned.1.call-done = bf16[1408,3,352]{2,1,0:T(4,128)(2,1)} async-done(((bf16[44,3,352]{2,1,0:T(4,128)(2,1)}), bf16[1408,3,352]{2,1,0:T(4,128)(2,1)}) %all-gather.9.cloned.1.call-update) | async-done | bytes 2973712 | tf_op jit(solution)/shard_map/all_gather | solution.py:64
  95.6 7.7 %copy.24 = bf16[1408,3,352]{0,2,1:T(8,128)(2,1)} copy(bf16[1408,3,352]{2,1,0:T(4,128)(2,1)} %all-gather.9.cloned.1.call-done) | data formatting | bytes 5947392 | tf_op jit(solution)/shard_map/all_gather | solution.py:64
  103.3 3.9 convolution_convert_fusion.2
  107.2 1.0 copy-done.4
  108.2 0.2 copy.35
  108.4 2.3 collective-permute-start
  110.8 0.9 copy.37
  111.7 1.3 collective-permute-start.1
  113.0 102.0 %all-gather = bf16[32,44,352]{2,1,0:T(8,128)(2,1)S(1)} all-gather(bf16[1,44,352]{2,1,0:T(8,128)(2,1)S(1)} %bitcast.53), channel_id=1, replica_groups=mesh['tm'=32,'tensor'=4] {'tm'}, dimensions={0}, use_global_device_ids=true | all-gather | bytes 1022208 | tf_op jit(solution)/shard_map/all_gather | solution.py:65
  215.0 1.2 reshape.90
  216.2 1.2 slice.31
  217.3 1.0 slice.34
  218.3 1.2 copy.36
  219.5 1.3 reshape.97
  220.8 1.4 pad_maximum_fusion
  222.2 2.3 reshape.72
  224.5 2.1 copy.28
  226.6 5.5 gather_fusion
  232.2 9.4 %copy.29 = bf16[64,64,2,4,88]{4,1,0,3,2:T(8,128)(2,1)} copy(bf16[64,64,2,4,88]{4,1,3,2,0:T(8,128)(2,1)} %gather_fusion) | data formatting | bytes 11534336 | tf_op jit(solution)/shard_map/while/body/eval_jaxpr/gather | solution.py:89
  241.5 5.9 fusion.110
  247.4 6.2 copy.40
  253.6 2.6 fusion.19
  256.2 2.8 fusion.112
  259.0 6.1 copy.38
  265.1 4.4 fusion.72
  269.5 0.4 copy.34
  270.0 0.4 reshape.74
  270.3 2.0 convolution_convert_fusion.1
  272.4 0.0 all-reduce.3.cloned.1.call-update
  272.4 0.0 all-gather.11.cloned.1.call-start
  272.4 0.7 all-gather.11.cloned.1.call-update
  273.1 0.0 all-gather.13.cloned.1.call-start
  273.2 0.5 all-gather.13.cloned.1.call-update
  273.7 0.0 all-gather.15.cloned.1.call-start
  273.7 0.5 all-gather.15.cloned.1.call-update
  274.3 0.3 all-reduce.5.cloned.1.call-start
  274.6 41.4 %all-reduce.3.cloned.1.call-done = bf16[512,1408]{1,0:T(8,128)(2,1)} async-done(((bf16[512,1408]{1,0:T(8,128)(2,1)}), bf16[512,1408]{1,0:T(8,128)(2,1)}) %all-reduce.3.cloned.1.call-update) | async-done | bytes 1441808 | tf_op jit(solution)/shard_map/psum | solution.py:54
  315.9 1.9 fusion.24
  317.9 0.6 multiply_reduce_fusion.1
  318.5 86.1 %all-gather.11.cloned.1.call-done = bf16[32,44,1536]{2,1,0:T(8,128)(2,1)} async-done(((bf16[1,44,1536]{2,1,0:T(8,128)(2,1)}), bf16[32,44,1536]{2,1,0:T(8,128)(2,1)}) %all-gather.11.cloned.1.call-update) | async-done | bytes 4325392 | tf_op jit(solution)/shard_map/all_gather | solution.py:66
  404.6 7.0 %reshape.92 = bf16[1408,1536]{1,0:T(8,128)(2,1)} reshape(bf16[32,44,1536]{2,1,0:T(8,128)(2,1)} %all-gather.11.cloned.1.call-done) | data formatting | bytes 8650752
  411.7 77.3 %all-gather.13.cloned.1.call-done = bf16[32,44,1536]{2,1,0:T(8,128)(2,1)} async-done(((bf16[1,44,1536]{2,1,0:T(8,128)(2,1)}), bf16[32,44,1536]{2,1,0:T(8,128)(2,1)}) %all-gather.13.cloned.1.call-update) | async-done | bytes 4325392 | tf_op jit(solution)/shard_map/all_gather | solution.py:67
  488.9 7.0 %reshape.94 = bf16[1408,1536]{1,0:T(8,128)(2,1)} reshape(bf16[32,44,1536]{2,1,0:T(8,128)(2,1)} %all-gather.13.cloned.1.call-done) | data formatting | bytes 8650752
  496.0 15.1 %convolution_convert_fusion = bf16[512,1408]{1,0:T(8,128)(2,1)} fusion(bf16[1408,1536]{1,0:T(8,128)(2,1)} %reshape.94, bf16[1408,1536]{1,0:T(8,128)(2,1)} %reshape.92, bf16[512,1408]{1,0:T(8,128)(2,1)S(1)} %copy-done.1, bf16[512,1408]{1,0:T(8,128)(2,1)S(1)} %copy-done, f32[1408]{0:T(1024)S(1)} %copy-done.9, f32[512]{0:T(512)S(1)} %add_rsqrt_fusion, ...), kind=kOutput, calls=%fused_computation.30 | convolution fusion | flops 4486070272 | bytes 12985856 | tf_op jit(solution)/shard_map/dot_general | solution.py:113
  511.0 0.0 all-reduce.5.cloned.1.call-update
  511.1 0.1 eq.47
  511.2 0.1 fusion.77
  511.2 0.2 reduce_window_sum.11
  511.4 0.2 select_reduce_fusion
  511.6 54.0 %all-gather.15.cloned.1.call-done = bf16[32,44,1024]{2,1,0:T(8,128)(2,1)} async-done(((bf16[1,44,1024]{2,1,0:T(8,128)(2,1)}), bf16[32,44,1024]{2,1,0:T(8,128)(2,1)}) %all-gather.15.cloned.1.call-update) | async-done | bytes 2883600 | tf_op jit(solution)/shard_map/all_gather | solution.py:68
  565.6 5.2 reshape.96
  570.8 40.6 %all-reduce.5.cloned.1.call-done = bf16[512,1408]{1,0:T(8,128)(2,1)} async-done(((bf16[512,1408]{1,0:T(8,128)(2,1)}), bf16[512,1408]{1,0:T(8,128)(2,1)}) %all-reduce.5.cloned.1.call-update) | async-done | bytes 1441808 | tf_op jit(solution)/shard_map/psum | solution.py:54
  611.5 1.8 convert_add_fusion.1
  613.3 1.1 fusion.23
  614.4 2.6 fusion.71
  617.0 23.1 %all_to_all.5 = bf16[32,8,1024]{2,1,0:T(8,128)(2,1)S(1)} all-to-all(bf16[32,8,1024]{2,1,0:T(8,128)(2,1)S(1)} %fusion.71), channel_id=1, replica_groups=mesh['tm'=32,'tensor'=4] {'tm'}, dimensions={0} | all-to-all | bytes 1048576 | tf_op jit(solution)/shard_map/all_to_all | solution.py:131
  640.1 0.8 copy.48
  (29 shorter events, 0.1 us)
Async XLA Ops:
  6.5 89.1 %all-gather.9.cloned.1.call-start = ((), (), s32[]{:S(2)}) async-start(), calls=%async_computation.1 | async-start | bytes 4460544 | tf_op jit(solution)/shard_map/all_gather | solution.py:64
  8.2 307.8 %all-reduce.3.cloned.1.call-start = ((), (), s32[]{:S(2)}) async-start(), calls=%async_computation.2 | async-start | bytes 2883584 | tf_op jit(solution)/shard_map/psum | solution.py:54
  12.5 90.8 %copy-start = (bf16[512,1408]{1,0:T(8,128)(2,1)S(1)}, bf16[512,1408]{1,0:T(8,128)(2,1)}, u32[]{:S(2)}) copy-start(bf16[512,1408]{1,0:T(8,128)(2,1)} %param.11) | copy-start | bytes 4325380
  12.5 90.8 %copy-start.8 = (f32[1408]{0:T(1024)S(1)}, f32[1408]{0:T(1024)}, u32[]{:S(2)}) copy-start(f32[1408]{0:T(1024)} %param.12) | copy-start | bytes 16900
  103.3 9.7 %copy-start.5 = (bf16[352,44]{0,1:T(8,128)(2,1)S(1)}, bf16[352,44]{0,1:T(8,128)(2,1)}, u32[]{:S(2)}) copy-start(bf16[352,44]{0,1:T(8,128)(2,1)} %param.14) | copy-start | bytes 92932
  107.2 1.0 copy-start.4
  108.4 112.3 %collective-permute-start = (bf16[256,2,352]{2,0,1:T(8,128)(2,1)S(1)}, bf16[256,2,352]{2,0,1:T(8,128)(2,1)S(1)}, u32[]{:S(2)}, u32[]{:S(2)}) collective-permute-start(bf16[256,2,352]{2,0,1:T(8,128)(2,1)S(1)} %copy.35), channel_id=1, source_target_pairs={{0,4},{4,8},{8,12},{12,16},{16,20},{20,24},{24,28},{28,32},{32,36}... | collective-permute-start | bytes 1081352 | tf_op jit(solution)/shard_map/ppermute | solution.py:21
  111.7 109.1 %collective-permute-start.1 = (bf16[256,2,352]{2,0,1:T(8,128)(2,1)}, bf16[256,2,352]{2,0,1:T(8,128)(2,1)}, u32[]{:S(2)}, u32[]{:S(2)}) collective-permute-start(bf16[256,2,352]{2,0,1:T(8,128)(2,1)} %copy.37), channel_id=1, source_target_pairs={{4,0},{8,4},{12,8},{16,12},{20,16},{24,20},{28,24},{32,28},{36,32}... | collective-permute-start | bytes 1081352 | tf_op jit(solution)/shard_map/ppermute | solution.py:24
  247.4 6.2 copy-start.2
  265.1 5.2 copy-start.3
  272.4 132.2 %all-gather.11.cloned.1.call-start = ((), (), s32[]{:S(2)}) async-start(), calls=%async_computation.4 | async-start | bytes 4866048 | tf_op jit(solution)/shard_map/all_gather | solution.py:66
  273.1 215.8 %all-gather.13.cloned.1.call-start = ((), (), s32[]{:S(2)}) async-start(), calls=%async_computation.5 | async-start | bytes 4866048 | tf_op jit(solution)/shard_map/all_gather | solution.py:67
  273.7 291.9 %all-gather.15.cloned.1.call-start = ((), (), s32[]{:S(2)}) async-start(), calls=%async_computation.6 | async-start | bytes 3244032 | tf_op jit(solution)/shard_map/all_gather | solution.py:68
  274.3 337.2 %all-reduce.5.cloned.1.call-start = ((), (), s32[]{:S(2)}) async-start(), calls=%async_computation.3 | async-start | bytes 2883584 | tf_op jit(solution)/shard_map/psum | solution.py:54
  315.9 1.9 copy-start.1
  411.7 84.3 %copy-start.9 = (f32[1408]{0:T(1024)S(1)}, f32[1408]{0:T(1024)}, u32[]{:S(2)}) copy-start(f32[1408]{0:T(1024)} %param.15) | copy-start | bytes 16900
  496.0 15.1 %copy-start.7 = (s32[512]{0:T(512)S(1)}, s32[512]{0:T(512)}, u32[]{:S(2)}) copy-start(s32[512]{0:T(512)} %param.20) | copy-start | bytes 6148
  496.0 15.2 %copy-start.6 = (s32[128,1]{0,1:T(1,128)S(1)}, s32[128,1]{0,1:T(1,128)}, u32[]{:S(2)}) copy-start(s32[128,1]{0,1:T(1,128)} %param.21) | copy-start | bytes 1540
Sparse Core Ops, SparseCore 0:
  10.3 85.2 all-gather.8
  272.5 43.3 all-reduce.2
  318.9 85.6 all-gather.10
  407.4 81.4 all-gather.12
  491.7 73.8 all-gather.14
  568.0 43.4 all-reduce.4
where the time goes:
time: 649 us; the launch traced here: 648 us
  waiting for transfers between devices  384 us (59%)
  blocking collectives  125 us (19%)
  local copies, waits for them, and re-layouts  75.8 us (12%)
  matrix products  31.7 us (5%)
  between operations  13.7 us (2%)
  other arithmetic  13.3 us (2%)
    all_gather x1, blocking collectives, body(): lax.all_gather(w_out, 'tm', axis=1, tiled=True)  102 us
    all_gather x1, waiting for transfers between devices, body(): lax.all_gather(w_up, 'tm', axis=0, tiled=True)  86.1 us
    all_gather x1, waiting for transfers between devices, body(): lax.all_gather(w_qkv, 'tm', axis=0, tiled=True)  83.1 us
    psum x2, waiting for transfers between devices, tensor_total(): return lax.psum(term.astype(jnp.bfloat16), 'tensor').astype(jnp.float32)  82 us
    all_gather x1, waiting for transfers between devices, body(): lax.all_gather(w_down, 'tm', axis=1, tiled=True)  77.3 us
    all_gather x1, waiting for transfers between devices, body(): lax.all_gather(w_proj, 'tm', axis=0, tiled=True)  54 us
    unnamed x31, local copies, waits for them, and re-layouts  38.5 us
    all_to_all x1, blocking collectives, body(): lax.all_to_all(outbox, 'tm', split_axis=0, concat_axis=0, tiled=True)  23.1 us
  transfers between devices with their start and end apart: 8, of which 6 were waited for; matrix products, arithmetic and copies ran while one was open for 7% of the time, Pallas kernels for 0%

commit v1 on v0

--- a/solution.py
+++ b/solution.py
@@ -60,8 +60,15 @@
     row_count = frames.shape[0]
     query_blocks = row_count // BLK
     head_dim = D // HEADS
+
+    def yards_drive(page, comm_axis):
+        plain = jnp.concatenate(
+            lax.all_to_all(jnp.stack(lax.axis_size(comm_axis) * [page]), comm_axis, 0, 0), axis=0
+        )
+        return plain
+
     full_qkv, full_out, full_up, full_down, full_proj = (
-        lax.all_gather(w_qkv, "tm", axis=0, tiled=True),
+        yards_drive(w_qkv, "tm"),
         lax.all_gather(w_out, "tm", axis=1, tiled=True),
         lax.all_gather(w_up, "tm", axis=0, tiled=True),
         lax.all_gather(w_down, "tm", axis=1, tiled=True),

time: 649 us -> 540 us (0.83)
  waiting for transfers between devices: 384 us -> 263 us
  starting transfers between devices: 4.01 us -> 15.9 us
  local copies, waits for them, and re-layouts: 75.8 us -> 84 us
    all_gather x1 -> x0, waiting for transfers between devices: 83.1 us -> none  [body(): lax.all_gather(w_qkv, 'tm', axis=0, tiled=True)]
    all_gather x1, waiting for transfers between devices: 86.1 us -> 35.9 us  [body(): lax.all_gather(w_up, 'tm', axis=0, tiled=True)]
    all_to_all x0 -> x1, waiting for transfers between devices: none -> 47.2 us  [yards_drive(): lax.all_to_all(jnp.stack(lax.axis_size(comm_axis) * [page]), comm_axis, 0...]
    psum x2, waiting for transfers between devices: 82 us -> 44.4 us  [tensor_total(): return lax.psum(term.astype(jnp.bfloat16), 'tensor').astype(jnp.float32)]
    another operation x0 -> x2, local copies, waits for them, and re-layouts: none -> 11.9 us  [the longest x1 8.92 us: body(): full_qkv.reshape(D, 3 * local_width)]
    all_to_all x0 -> x1, starting transfers between devices: none -> 11 us  [yards_drive(): lax.all_to_all(jnp.stack(lax.axis_size(comm_axis) * [page]), comm_axis, 0...]
    all_gather x1 -> x0, local copies, waits for them, and re-layouts: 7.69 us -> none  [body(): lax.all_gather(w_qkv, 'tm', axis=0, tiled=True)]
    unnamed x31 -> x32, local copies, waits for them, and re-layouts: 38.5 us -> 36.9 us
  transfers between devices with their start and end apart: 8 -> 8, of which waited for: 6 -> 5; matrix products, arithmetic and copies ran while one was open for 7% -> 8% of each run, Pallas kernels for 0% -> 0%
where the time goes in v1:
time: 540 us; the launch traced here: 539 us
  waiting for transfers between devices  263 us (49%)
  blocking collectives  119 us (22%)
  local copies, waits for them, and re-layouts  84 us (16%)
  matrix products  31.8 us (6%)
  starting transfers between devices  15.9 us (3%)
  between operations  15.2 us (3%)
  other arithmetic  9.91 us (2%)
    all_gather x1, blocking collectives, body(): lax.all_gather(w_out, 'tm', axis=1, tiled=True)  102 us
    all_gather x1, waiting for transfers between devices, body(): lax.all_gather(w_down, 'tm', axis=1, tiled=True)  77.2 us
    all_gather x1, waiting for transfers between devices, body(): lax.all_gather(w_proj, 'tm', axis=0, tiled=True)  56.6 us
    all_to_all x1, waiting for transfers between devices, yards_drive(): lax.all_to_all(jnp.stack(lax.axis_size(comm_axis) * [page]), comm_axis, 0...  47.2 us
    psum x2, waiting for transfers between devices, tensor_total(): return lax.psum(term.astype(jnp.bfloat16), 'tensor').astype(jnp.float32)  44.4 us
    unnamed x32, local copies, waits for them, and re-layouts  36.9 us
    all_gather x1, waiting for transfers between devices, body(): lax.all_gather(w_up, 'tm', axis=0, tiled=True)  35.9 us
    all_to_all x1, blocking collectives, body(): lax.all_to_all(outbox, 'tm', split_axis=0, concat_axis=0, tiled=True)  17 us
  transfers between devices with their start and end apart: 8, of which 5 were waited for; matrix products, arithmetic and copies ran while one was open for 8% of the time, Pallas kernels for 0%

profile of v1, /device:TPU:0, one launch (start us, length us, event | category | flops | bytes accessed | tf_op | source)
XLA Modules:
  0.0 538.6 jit_solution(12738173939977438523)
XLA Ops:
  7.4 2.9 stack.2
  10.3 11.0 %all-to-all-start = ((bf16[32,44,3,352]{3,1,2,0:T(8,128)(2,1)}), bf16[32,44,3,352]{3,1,2,0:T(8,128)(2,1)}, u32[]{:S(2)}, u32[]{:S(2)}) async-start(bf16[32,44,3,352]{3,1,2,0:T(8,128)(2,1)} %stack.2), calls=%async_computation | async-start | bytes 7077888 | tf_op jit(solution)/shard_map/all_to_all | solution.py:66
  21.3 0.0 all-reduce.3.cloned.1.call-start
  21.4 0.1 reshape.78
  21.5 0.3 convert_reduce_fusion
  21.7 0.5 fusion.16
  22.3 47.2 %all-to-all-done = bf16[32,44,3,352]{3,1,2,0:T(8,128)(2,1)} async-done(((bf16[32,44,3,352]{3,1,2,0:T(8,128)(2,1)}), bf16[32,44,3,352]{3,1,2,0:T(8,128)(2,1)}, u32[]{:S(2)}, u32[]{:S(2)}) %all-to-all-start) | async-done | bytes 2973728 | tf_op jit(solution)/shard_map/all_to_all | solution.py:66
  69.5 5.7 %copy.24 = bf16[32,44,3,352]{3,2,1,0:T(4,128)(2,1)} copy(bf16[32,44,3,352]{3,1,2,0:T(8,128)(2,1)} %all-to-all-done) | data formatting | bytes 5947392 | tf_op jit(solution)/shard_map/all_to_all | solution.py:66
  75.2 8.9 %reshape_reshape.3 = bf16[1408,1056]{1,0:T(8,128)(2,1)} reshape(bf16[32,44,3,352]{3,2,1,0:T(4,128)(2,1)} %copy.24) | data formatting | bytes 5947392 | tf_op jit(solution)/shard_map/reshape;reshape | solution.py:81
  84.1 4.0 convolution_convert_fusion
  88.1 1.0 copy-done.4
  89.1 0.2 copy.35
  89.4 3.2 collective-permute-start
  92.6 0.9 copy.37
  93.5 1.3 collective-permute-start.1
  94.8 101.8 %all-gather = bf16[32,44,352]{2,1,0:T(8,128)(2,1)S(1)} all-gather(bf16[1,44,352]{2,1,0:T(8,128)(2,1)S(1)} %bitcast.51), channel_id=1, replica_groups=mesh['tm'=32,'tensor'=4] {'tm'}, dimensions={0}, use_global_device_ids=true | all-gather | bytes 1022208 | tf_op jit(solution)/shard_map/all_gather | solution.py:72
  196.7 1.2 reshape.88
  197.9 1.2 slice.31
  199.0 1.0 slice.34
  200.0 1.2 copy.36
  201.2 1.3 reshape.95
  202.5 0.0 collective-permute-done
  202.5 1.4 pad_maximum_fusion
  203.9 2.3 reshape.70
  206.2 2.1 copy.28
  208.3 5.5 %gather_fusion = bf16[64,64,2,4,88]{4,1,3,2,0:T(8,128)(2,1)} fusion(bf16[16,64,2,4,88]{4,1,3,2,0:T(8,128)(2,1)S(1)} %copy.28, s32[1024]{0:T(1024)S(1)} %pad_clamp_fusion), kind=kCustom, calls=%fused_computation | custom fusion | bytes 11534592 | tf_op jit(solution)/shard_map/while/body/eval_jaxpr/gather | solution.py:96
  213.9 9.4 %copy.29 = bf16[64,64,2,4,88]{4,1,0,3,2:T(8,128)(2,1)} copy(bf16[64,64,2,4,88]{4,1,3,2,0:T(8,128)(2,1)} %gather_fusion) | data formatting | bytes 11534336 | tf_op jit(solution)/shard_map/while/body/eval_jaxpr/gather | solution.py:96
  223.2 5.9 %fusion.110 = (bf16[8,512,1,4,88]{4,1,0,3,2:T(8,128)(2,1)}, bf16[8,512,1,4,88]{4,1,0,3,2:T(8,128)(2,1)}) fusion(bf16[8,512,2,4,88]{4,1,0,3,2:T(8,128)(2,1)} %bitcast.41), kind=kLoop, calls=%fused_computation.136 | loop fusion | bytes 11534336 | tf_op jit(solution)/shard_map/while/body/eval_jaxpr/slice | solution.py:107
  229.1 6.2 %copy.40 = bf16[8,512,1,4,88]{1,4,3,0,2:T(8,128)(2,1)} copy(bf16[8,512,1,4,88]{4,1,0,3,2:T(8,128)(2,1)} %get-tuple-element.14) | data formatting | bytes 5767168
  235.3 2.6 fusion.19
  237.9 2.8 fusion.112
  240.7 6.1 %copy.38 = bf16[8,512,1,4,88]{1,4,3,0,2:T(8,128)(2,1)} copy(bf16[8,512,1,4,88]{4,1,0,3,2:T(8,128)(2,1)} %get-tuple-element.13) | data formatting | bytes 5767168
  246.8 4.4 fusion.72
  251.2 0.4 copy.34
  251.6 0.4 reshape.72
  252.0 2.0 convolution_convert_fusion.2
  254.1 0.0 all-reduce.3.cloned.1.call-update
  254.1 0.0 all-gather.8.cloned.1.call-start
  254.1 0.5 all-gather.8.cloned.1.call-update
  254.7 0.0 all-gather.10.cloned.1.call-start
  254.7 0.5 all-gather.10.cloned.1.call-update
  255.3 0.0 all-gather.12.cloned.1.call-start
  255.3 0.5 all-gather.12.cloned.1.call-update
  255.8 0.3 all-reduce.5.cloned.1.call-start
  256.1 44.4 %all-reduce.3.cloned.1.call-done = bf16[512,1408]{1,0:T(8,128)(2,1)} async-done(((bf16[512,1408]{1,0:T(8,128)(2,1)}), bf16[512,1408]{1,0:T(8,128)(2,1)}) %all-reduce.3.cloned.1.call-update) | async-done | bytes 1441808 | tf_op jit(solution)/shard_map/psum | solution.py:54
  300.5 1.9 fusion.24
  302.4 0.6 multiply_reduce_fusion.1
  303.1 35.9 %all-gather.8.cloned.1.call-done = bf16[32,44,1536]{2,1,0:T(8,128)(2,1)} async-done(((bf16[1,44,1536]{2,1,0:T(8,128)(2,1)}), bf16[32,44,1536]{2,1,0:T(8,128)(2,1)}) %all-gather.8.cloned.1.call-update) | async-done | bytes 4325392 | tf_op jit(solution)/shard_map/all_gather | solution.py:73
  339.0 7.0 %reshape.90 = bf16[1408,1536]{1,0:T(8,128)(2,1)} reshape(bf16[32,44,1536]{2,1,0:T(8,128)(2,1)} %all-gather.8.cloned.1.call-done) | data formatting | bytes 8650752
  346.0 77.2 %all-gather.10.cloned.1.call-done = bf16[32,44,1536]{2,1,0:T(8,128)(2,1)} async-done(((bf16[1,44,1536]{2,1,0:T(8,128)(2,1)}), bf16[32,44,1536]{2,1,0:T(8,128)(2,1)}) %all-gather.10.cloned.1.call-update) | async-done | bytes 4325392 | tf_op jit(solution)/shard_map/all_gather | solution.py:74
  423.2 7.0 %reshape.92 = bf16[1408,1536]{1,0:T(8,128)(2,1)} reshape(bf16[32,44,1536]{2,1,0:T(8,128)(2,1)} %all-gather.10.cloned.1.call-done) | data formatting | bytes 8650752
  430.3 15.1 %convolution_convert_fusion.1 = bf16[512,1408]{1,0:T(8,128)(2,1)} fusion(bf16[1408,1536]{1,0:T(8,128)(2,1)} %reshape.92, bf16[1408,1536]{1,0:T(8,128)(2,1)} %reshape.90, bf16[512,1408]{1,0:T(8,128)(2,1)S(1)} %copy-done.1, bf16[512,1408]{1,0:T(8,128)(2,1)S(1)} %copy-done, f32[1408]{0:T(1024)S(1)} %copy-done.10, f32[512]{0:T(512)S(1)} %add_rsqrt_fusion, ...), kind=kOutput, calls=%fused_computation.31 | convolution fusion | flops 4486070272 | bytes 12985856 | tf_op jit(solution)/shard_map/dot_general | solution.py:120
  445.3 0.0 all-reduce.5.cloned.1.call-update
  445.4 0.1 eq.47
  445.4 0.1 fusion.77
  445.5 0.2 reduce_window_sum.11
  445.7 0.2 select_reduce_fusion
  445.9 56.6 %all-gather.12.cloned.1.call-done = bf16[32,44,1024]{2,1,0:T(8,128)(2,1)} async-done(((bf16[1,44,1024]{2,1,0:T(8,128)(2,1)}), bf16[32,44,1024]{2,1,0:T(8,128)(2,1)}) %all-gather.12.cloned.1.call-update) | async-done | bytes 2883600 | tf_op jit(solution)/shard_map/all_gather | solution.py:75
  502.4 5.2 reshape.94
  507.7 1.8 convert_add_fusion.1
  509.5 1.1 fusion.23
  510.6 2.6 fusion.71
  513.2 17.0 %all_to_all.10 = bf16[32,8,1024]{2,1,0:T(8,128)(2,1)S(1)} all-to-all(bf16[32,8,1024]{2,1,0:T(8,128)(2,1)S(1)} %fusion.71), channel_id=1, replica_groups=mesh['tm'=32,'tensor'=4] {'tm'}, dimensions={0} | all-to-all | bytes 1048576 | tf_op jit(solution)/shard_map/all_to_all | solution.py:138
  530.2 0.8 copy.48
  (31 shorter events, 0.1 us)
Async XLA Ops:
  10.3 11.1 %copy-start.6 = (s32[8,8]{1,0:T(8,128)S(1)}, s32[8,8]{1,0:T(8,128)}, u32[]{:S(2)}) copy-start(s32[8,8]{1,0:T(8,128)} %param.19) | copy-start | bytes 772
  10.3 11.2 %copy-start = (bf16[512,1408]{1,0:T(8,128)(2,1)S(1)}, bf16[512,1408]{1,0:T(8,128)(2,1)}, u32[]{:S(2)}) copy-start(bf16[512,1408]{1,0:T(8,128)(2,1)} %param.11) | copy-start | bytes 4325380
  10.3 59.2 %all-to-all-start = ((bf16[32,44,3,352]{3,1,2,0:T(8,128)(2,1)}), bf16[32,44,3,352]{3,1,2,0:T(8,128)(2,1)}, u32[]{:S(2)}, u32[]{:S(2)}) async-start(bf16[32,44,3,352]{3,1,2,0:T(8,128)(2,1)} %stack.2), calls=%async_computation | async-start | bytes 7077888 | tf_op jit(solution)/shard_map/all_to_all | solution.py:66
  21.3 279.1 %all-reduce.3.cloned.1.call-start = ((), (), s32[]{:S(2)}) async-start(), calls=%async_computation.2 | async-start | bytes 2883584 | tf_op jit(solution)/shard_map/psum | solution.py:54
  75.2 8.9 %copy-start.9 = (f32[1408]{0:T(1024)S(1)}, f32[1408]{0:T(1024)}, u32[]{:S(2)}) copy-start(f32[1408]{0:T(1024)} %param.12) | copy-start | bytes 16900
  84.1 10.7 %copy-start.5 = (bf16[352,44]{0,1:T(8,128)(2,1)S(1)}, bf16[352,44]{0,1:T(8,128)(2,1)}, u32[]{:S(2)}) copy-start(bf16[352,44]{0,1:T(8,128)(2,1)} %param.14) | copy-start | bytes 92932
  88.1 1.0 copy-start.4
  89.4 113.1 %collective-permute-start = (bf16[256,2,352]{2,0,1:T(8,128)(2,1)S(1)}, bf16[256,2,352]{2,0,1:T(8,128)(2,1)S(1)}, u32[]{:S(2)}, u32[]{:S(2)}) collective-permute-start(bf16[256,2,352]{2,0,1:T(8,128)(2,1)S(1)} %copy.35), channel_id=1, source_target_pairs={{0,4},{4,8},{8,12},{12,16},{16,20},{20,24},{24,28},{28,32},{32,36}... | collective-permute-start | bytes 1081352 | tf_op jit(solution)/shard_map/ppermute | solution.py:21
  93.5 109.0 %collective-permute-start.1 = (bf16[256,2,352]{2,0,1:T(8,128)(2,1)}, bf16[256,2,352]{2,0,1:T(8,128)(2,1)}, u32[]{:S(2)}, u32[]{:S(2)}) collective-permute-start(bf16[256,2,352]{2,0,1:T(8,128)(2,1)} %copy.37), channel_id=1, source_target_pairs={{4,0},{8,4},{12,8},{16,12},{20,16},{24,20},{28,24},{32,28},{36,32}... | collective-permute-start | bytes 1081352 | tf_op jit(solution)/shard_map/ppermute | solution.py:24
  229.1 6.2 %copy-start.2 = (bf16[8,64,4,88]{1,0,3,2:T(8,128)(2,1)S(1)}, bf16[8,64,4,88]{1,0,3,2:T(8,128)(2,1)}, u32[]{:S(2)}) copy-start(bf16[8,64,4,88]{1,0,3,2:T(8,128)(2,1)} %reshape.95) | copy-start | bytes 1081348
  246.8 5.2 copy-start.3
  254.1 84.9 %all-gather.8.cloned.1.call-start = ((), (), s32[]{:S(2)}) async-start(), calls=%async_computation.4 | async-start | bytes 4866048 | tf_op jit(solution)/shard_map/all_gather | solution.py:73
  254.7 168.6 %all-gather.10.cloned.1.call-start = ((), (), s32[]{:S(2)}) async-start(), calls=%async_computation.5 | async-start | bytes 4866048 | tf_op jit(solution)/shard_map/all_gather | solution.py:74
  255.3 247.2 %all-gather.12.cloned.1.call-start = ((), (), s32[]{:S(2)}) async-start(), calls=%async_computation.6 | async-start | bytes 3244032 | tf_op jit(solution)/shard_map/all_gather | solution.py:75
  255.8 251.9 %all-reduce.5.cloned.1.call-start = ((), (), s32[]{:S(2)}) async-start(), calls=%async_computation.3 | async-start | bytes 2883584 | tf_op jit(solution)/shard_map/psum | solution.py:54
  300.5 1.9 copy-start.1
  346.0 84.2 %copy-start.10 = (f32[1408]{0:T(1024)S(1)}, f32[1408]{0:T(1024)}, u32[]{:S(2)}) copy-start(f32[1408]{0:T(1024)} %param.15) | copy-start | bytes 16900
  430.2 15.1 %copy-start.8 = (s32[512]{0:T(512)S(1)}, s32[512]{0:T(512)}, u32[]{:S(2)}) copy-start(s32[512]{0:T(512)} %param.20) | copy-start | bytes 6148
  430.2 15.2 %copy-start.7 = (s32[128,1]{0,1:T(1,128)S(1)}, s32[128,1]{0,1:T(1,128)}, u32[]{:S(2)}) copy-start(s32[128,1]{0,1:T(1,128)} %param.21) | copy-start | bytes 1540
Sparse Core Ops, SparseCore 0:
  254.2 46.2 all-reduce.2
  445.5 55.9 all-reduce.4
Sparse Core Ops, SparseCore 1:
  257.5 81.4 all-gather.7
  341.8 81.4 all-gather.9
  426.1 76.3 all-gather.11
